TPU v7x, 512 devices: a whole 4x4x16 slice. The times are simulated.
512 devices in a mesh: dp: 16 (over z), tensor: 32 (over y, x, core).
Axes of the slice: x: 4, y: 4, z: 16, core: 2. Of those that a mesh axis runs over, the one named last changes fastest.
Arguments:
- acts: bfloat16 [16, 512, 4096], P('dp', None, 'tensor'), may hold values from -6 to 6
- grads: bfloat16 [16, 512, 4096], P('dp', None, 'tensor'), may hold values from -6 to 6
- basis_in_held: bfloat16 [16, 4096, 4096], P('dp', None, 'tensor'), may hold values from -0.09375 to 0.09375
- basis_out_held: bfloat16 [16, 4096, 4096], P('dp', None, 'tensor'), may hold values from -0.09375 to 0.09375
- owners: int32 [2, 32], replicated, may hold values from 0 to 15
- eig_lambda: bfloat16 [4096, 4096], P('tensor'), may hold values from 0.0049743652 to 0.19921875
Outputs:
- precond: bfloat16 [16, 4096, 4096], P('dp', 'tensor')
Inputs may be any that keep to these rules, and one draw needn't show every extreme that they name: `owners`: row 0 is for the input eigenbasis, row 1 for the output eigenbasis; entry j names the dp group whose copy of column block j is current, the other copies of that block are stale.
All inputs are finite; a program needn't handle non-finite values.
Results may differ from a plain program's by a relative error of at most 0.0057.
Values may be sent and summed in bfloat16 or wider, within the bound.
A program may use at most 64 MiB of HBM per device.

v0:
```python
import jax
import jax.numpy as jnp
from jax import lax
from jax.sharding import PartitionSpec as P

damping = 0.01


def from_root(block, axis, owner):
    block = jnp.where(lax.axis_index(axis) == owner, block, jnp.zeros_like(block))
    return lax.psum(block, axis)


def shards(acts, grads, basis_in_held, basis_out_held, owners, eig_lambda):
    column = lax.axis_index("tensor")
    owner_in = owners[0, column]
    owner_out = owners[1, column]
    basis_in = from_root(basis_in_held[0], "dp", owner_in)
    basis_out = from_root(basis_out_held[0], "dp", owner_out)
    tokens = acts.shape[1]
    rot_in = jnp.dot(
        lax.all_gather(acts[0], "tensor", axis=1, tiled=True),
        basis_in,
        preferred_element_type=jnp.float32,
    )
    rot_out = jnp.dot(
        lax.all_gather(grads[0], "tensor", axis=1, tiled=True),
        basis_out,
        preferred_element_type=jnp.float32,
    )
    rot_in = rot_in.astype(jnp.bfloat16)
    rot_out = rot_out.astype(jnp.bfloat16)
    denom = eig_lambda.astype(jnp.float32) + damping
    contract = (((0,), (0,)), ((), ()))
    product = (
        lax.dot_general(
            rot_out,
            lax.all_gather(rot_in, "tensor", axis=1, tiled=True),
            contract,
            preferred_element_type=jnp.float32,
        )
        / tokens
    )
    return (product / denom).astype(jnp.bfloat16)[None]


def solution(mesh):
    placed = (
        P("dp", None, "tensor"),
        P("dp", None, "tensor"),
        P("dp", None, "tensor"),
        P("dp", None, "tensor"),
        P(),
        P("tensor", None),
    )
    return jax.shard_map(
        shards, mesh=mesh, in_specs=placed, out_specs=P("dp", "tensor", None), check_vma=False
    )
```

profile of v0, /device:TPU:1, one launch (start us, length us, event | category | flops | bytes accessed | tf_op | source)
XLA Modules:
  0.0 240.1 jit_solution(7664022337786298298)
XLA Ops:
  7.4 0.0 all-reduce.3.cloned.1.call-start
  7.4 1.4 constant_dynamic-slice_fusion
  10.0 1.5 select_bitcast_fusion
  11.5 0.0 copy-start
  11.5 0.0 all-reduce.3.cloned.1.call-update
  11.6 0.0 all-gather.10.cloned.1.call-start
  11.6 0.5 all-gather.10.cloned.1.call-update
  12.1 0.0 all-gather.8.cloned.1.call-start
  12.2 0.5 all-gather.8.cloned.1.call-update
  12.7 0.0 all-gather.6.cloned.1.call-start
  12.8 140.7 %all-reduce.3.cloned.1.call-done = (bf16[4096,128]{1,0:T(8,128)(2,1)}, bf16[4096,128]{1,0:T(8,128)(2,1)}) async-done(((bf16[4096,128]{1,0:T(8,128)(2,1)}, bf16[4096,128]{1,0:T(8,128)(2,1)}), (bf16[4096,128]{1,0:T(8,128)(2,1)}, bf16[4096,128]{1,0:T(8,128)(2,1)})) %all-reduce.3.cloned.1.call-update) | async-done | bytes 2097168 | tf_op jit(solution)/shard_map/psum | solution.py:11
  153.5 0.0 copy-start.1
  153.5 0.0 all-gather.10.cloned.1.call-done
  153.5 4.8 %fusion.13 = bf16[512,128]{0,1:T(8,128)(2,1)} fusion(bf16[4096,128]{1,0:T(8,128)(2,1)} %get-tuple-element.5, bf16[1,512,4096]{2,1,0:T(8,128)(2,1)} %all-gather.10.cloned.1.call-done), kind=kOutput, calls=%fused_computation.10 | convolution fusion | flops 536936448 | bytes 5373952 | tf_op jit(solution)/shard_map/dot_general | solution.py:21
  158.2 0.0 all-gather.6.cloned.1.call-update
  158.3 0.0 all-gather.8.cloned.1.call-done
  158.3 66.8 %all-gather.6.cloned.1.call-done = bf16[512,4096]{0,1:T(8,128)(2,1)} async-done(((bf16[512,128]{0,1:T(8,128)(2,1)}), bf16[512,4096]{0,1:T(8,128)(2,1)}) %all-gather.6.cloned.1.call-update) | async-done | bytes 4194320 | tf_op jit(solution)/shard_map/all_gather | solution.py:38
  225.1 0.0 copy-done
  225.1 0.0 copy-done.1
  225.1 7.4 %fusion.2 = bf16[1,128,4096]{2,1,0:T(8,128)(2,1)} fusion(bf16[512,4096]{0,1:T(8,128)(2,1)} %all-gather.6.cloned.1.call-done, bf16[128,4096]{1,0:T(8,128)(2,1)S(1)} %copy-done, bf16[4096,128]{1,0:T(8,128)(2,1)S(1)} %copy-done.1, bf16[1,512,4096]{2,1,0:T(8,128)(2,1)} %all-gather.8.cloned.1.call-done), kind=kOutput, calls=%fused_computation.3 | convolution fusion | flops 1076428800 | bytes 11534336 | tf_op jit(solution)/shard_map/dot_general | solution.py:36
Async XLA Ops:
  7.4 146.1 %all-reduce.3.cloned.1.call-start = ((), (), s32[]{:S(2)}) async-start(), calls=%async_computation.3 | async-start | bytes 4194304 | tf_op jit(solution)/shard_map/psum | solution.py:11
  11.5 213.6 %copy-start = (bf16[128,4096]{1,0:T(8,128)(2,1)S(1)}, bf16[128,4096]{1,0:T(8,128)(2,1)}, u32[]{:S(2)}) copy-start(bf16[128,4096]{1,0:T(8,128)(2,1)} %param.11) | copy-start | bytes 3145732
  11.6 141.9 %all-gather.10.cloned.1.call-start = ((), (), s32[]{:S(2)}) async-start(), calls=%async_computation.2 | async-start | bytes 4325376 | tf_op jit(solution)/shard_map/all_gather | solution.py:22
  12.1 146.1 %all-gather.8.cloned.1.call-start = ((), (), s32[]{:S(2)}) async-start(), calls=%async_computation.1 | async-start | bytes 4325376 | tf_op jit(solution)/shard_map/all_gather | solution.py:27
  12.7 212.4 %all-gather.6.cloned.1.call-start = ((), (), s32[]{:S(2)}) async-start(), calls=%async_computation | async-start | bytes 4325376 | tf_op jit(solution)/shard_map/all_gather | solution.py:38
  153.5 71.7 %copy-start.1 = (bf16[4096,128]{1,0:T(8,128)(2,1)S(1)}, bf16[4096,128]{1,0:T(8,128)(2,1)}, u32[]{:S(2)}) copy-start(bf16[4096,128]{1,0:T(8,128)(2,1)} %get-tuple-element.6) | copy-start | bytes 3145732
Sparse Core Ops, SparseCore 0:
  11.7 141.7 all-reduce.2
Sparse Core Ops, SparseCore 1:
  15.1 70.2 all-gather.9
  88.3 63.4 all-gather.7
  158.3 66.7 all-gather.5
where the time goes:
time: 240 us
  waiting for transfers between devices  209 us (87%)
  between operations  16.3 us (7%)
  matrix products  12.1 us (5%)
    psum x1, waiting for transfers between devices, from_root(): return lax.psum(block, axis)  141 us
    all_gather x1, waiting for transfers between devices, shards(): lax.all_gather(rot_in, 'tensor', axis=1, tiled=True)  66.8 us
    dot_general x1, matrix products, shards(): lax.dot_general(rot_out, lax.all_gather(rot_in, 'tensor', axis=1, tiled=T...  7.36 us
  transfers between devices with their start and end apart: 4, of which 2 were waited for; matrix products, arithmetic and copies ran while one was open for 2% of the time, Pallas kernels for 0%

commit v1 on v0

v1 whole, which is shorter than its diff:
```python
import functools

import jax
import jax.numpy as jnp
from jax import lax
from jax.experimental import pallas as pl
from jax.experimental.pallas import tpu as pltpu
from jax.sharding import PartitionSpec as P

damping = 0.01
MESH = pl.DeviceIdType.MESH
NX = 4
NY = 4
SUBS = 2
ALL = slice(None)


class Slots:
    def __init__(self, sems):
        self.sems = sems
        self.used = 0

    def take(self):
        self.used += 1
        return self.sems.at[self.used - 1]


class Plane:
    def __init__(self, buf, where, to, send, recv):
        self.buf, self.to, self.send, self.recv = buf, to, send, recv
        self.y, self.x, self.c = where
        self.landing = {}
        self.sent = []
        self.partner = []

    def at(self, dx, dy, part, core=None):
        y = lax.rem(self.y + (dy % NY), NY)
        x = lax.rem(self.x + (dx % NX), NX)
        return self.buf.at[(y, x, self.c if core is None else core) + part]

    def push(self, way, dx, dy, part):
        wx, wy = {"+x": (1, 0), "-x": (-1, 0), "+y": (0, 1), "-y": (0, -1)}[way]
        region = self.at(dx, dy, part)
        recv = self.recv.take()
        copy = pltpu.make_async_remote_copy(
            region, region, self.send.take(), recv, device_id=self.to[way], device_id_type=MESH
        )
        copy.start()
        self.sent.append(copy)
        lands = self.at(dx - wx, dy - wy, part)
        self.landing[(way, (dx - wx) % NX, (dy - wy) % NY, str(part))] = pltpu.make_async_remote_copy(
            lands, lands, self.send.sems.at[0], recv, device_id=self.to[way], device_id_type=MESH
        )

    def arrive(self, way, dx, dy, part):
        self.landing.pop((way, dx % NX, dy % NY, str(part))).wait_recv()

    def share(self, dx, dy):
        region = self.at(dx, dy, ())
        recv = self.recv.take()
        copy = pltpu.make_async_remote_copy(
            region, region, self.send.take(), recv, device_id=self.to["core"], device_id_type=MESH
        )
        copy.start()
        self.sent.append(copy)
        lands = self.at(dx, dy, (), 1 - self.c)
        self.partner.append(
            pltpu.make_async_remote_copy(
                lands, lands, self.send.sems.at[0], recv, device_id=self.to["core"], device_id_type=MESH
            )
        )

    def waves(self):
        return [self.wave1, self.wave2, self.wave3, self.wave4, self.wave5, self.wave6]

    def wave1(self):
        for way in ("+x", "-x", "+y", "-y"):
            self.push(way, 0, 0, ())
        self.share(0, 0)

    def wave2(self):
        top, bottom = (ALL, 0), (ALL, 1)
        for way, dx, dy, part, half, across in (
            ("+x", -1, 0, top, (0,), ("+y", "-y")),
            ("-x", 1, 0, bottom, (0,), ("+y", "-y")),
            ("+y", 0, -1, top, (1,), ("+x", "-x")),
            ("-y", 0, 1, bottom, (1,), ("+x", "-x")),
        ):
            self.arrive(way, dx, dy, ())
            self.push(way, dx, dy, part)
            for side in across:
                self.push(side, dx, dy, half)
            self.share(dx, dy)

    def wave3(self):
        top, bottom = (ALL, 0), (ALL, 1)
        self.arrive("+x", 2, 0, top)
        self.arrive("-x", 2, 0, bottom)
        self.push("+y", 2, 0, (0,))
        self.push("-y", 2, 0, (0,))
        self.arrive("+y", 0, 2, top)
        self.arrive("-y", 0, 2, bottom)
        self.push("+x", 0, 2, (1,))
        self.push("-x", 0, 2, (1,))
        for way, dx, dy, part, on in (
            ("+y", -1, -1, (0,), (0, 0)),
            ("+y", 1, -1, (0,), (0, 0)),
            ("-y", -1, 1, (0,), (0, 1)),
            ("-y", 1, 1, (0,), (0, 1)),
            ("+x", -1, -1, (1,), (1, 0)),
            ("+x", -1, 1, (1,), (1, 0)),
            ("-x", 1, -1, (1,), (1, 1)),
            ("-x", 1, 1, (1,), (1, 1)),
        ):
            self.arrive(way, dx, dy, part)
            self.push(way, dx, dy, on)
        for dx, dy in ((2, 0), (0, 2), (-1, -1), (1, -1), (-1, 1), (1, 1)):
            self.share(dx, dy)

    def wave4(self):
        for way, dx, dy, part, on in (
            ("+y", 2, -1, (0,), (0, 0)),
            ("-y", 2, 1, (0,), (0, 1)),
            ("+x", -1, 2, (1,), (1, 0)),
            ("-x", 1, 2, (1,), (1, 1)),
        ):
            self.arrive(way, dx, dy, part)
            self.push(way, dx, dy, on)
        for far in (-1, 1):
            self.arrive("+y", far, 2, (0, 0))
            self.arrive("-y", far, 2, (0, 1))
            self.arrive("+x", 2, far, (1, 0))
            self.arrive("-x", 2, far, (1, 1))
        for dx, dy in ((-1, 2), (1, 2), (2, -1), (2, 1)):
            self.share(dx, dy)

    def wave5(self):
        self.arrive("+y", 2, 2, (0, 0))
        self.arrive("-y", 2, 2, (0, 1))
        self.arrive("+x", 2, 2, (1, 0))
        self.arrive("-x", 2, 2, (1, 1))
        self.share(2, 2)
        assert not self.landing

    def wave6(self):
        for copy in self.partner:
            copy.wait_recv()

    def drain(self):
        for copy in self.sent:
            copy.wait_send()


class Ring:
    def __init__(self, n, z, held, full, got, owner, up, down, send, recv, landed):
        self.n, self.z, self.held, self.full, self.got = n, z, held, full, got
        self.owner, self.to = owner, (up, down)
        self.hops = (n // 2, n // 2 - 1)
        self.landed = landed
        self.recv = [[[recv.take() for _ in range(SUBS)] for _ in range(2 * h)] for h in self.hops]
        self.send = [[send.take() for _ in range(SUBS)] for _ in range(2)]
        self.flying = {}

    def wrap(self, p):
        return lax.rem(p + 4 * self.n, self.n)

    def go(self, side, step, sub, src, dst):
        if (side, sub) in self.flying:
            self.flying.pop((side, sub)).wait_send()
        copy = pltpu.make_async_remote_copy(
            src,
            dst,
            self.send[side][sub],
            self.recv[side][step][sub],
            device_id=self.to[side],
            device_id_type=MESH,
        )
        copy.start()
        self.flying[(side, sub)] = copy

    def came(self, side, step, sub, where):
        pltpu.make_async_remote_copy(
            where,
            where,
            self.send[side][sub],
            self.recv[side][step][sub],
            device_id=self.to[side],
            device_id_type=MESH,
        ).wait_recv()

    def slot(self, side, step, sub):
        return self.got.at[side * self.hops[0] + step, sub]

    def piece_out(self, side, step):
        h = self.hops[side]
        return self.wrap(self.z + h - step if side == 0 else self.z - h + step)

    def step(self, k):
        h0 = self.hops[0]
        mine = self.owner == self.z
        for sub in range(SUBS):
            for side in (0, 1):
                h = self.hops[side]
                if k < h:
                    src = self.held.at[self.piece_out(side, k), sub]
                    if k > 0:
                        slot = self.slot(side, k - 1, sub)
                        self.came(side, k - 1, sub, slot)
                        slot[...] = jnp.where(mine, src[...], slot[...])
                        src = slot
                    self.go(side, k, sub, src, self.slot(side, k, sub))
                elif k < h0:
                    self.came(side, k - 1, sub, self.slot(side, k - 1, sub))
            if k == h0:
                self.came(0, k - 1, sub, self.slot(0, k - 1, sub))
                if self.hops[1] == h0:
                    self.came(1, k - 1, sub, self.slot(1, k - 1, sub))
                back = self.z - self.owner
                back = jnp.where(back < 0, back + self.n, back)
                here = self.full.at[self.z, sub]
                above = self.slot(1, self.hops[1] - 1, sub)[...]
                below = self.slot(0, h0 - 1, sub)[...]
                other = jnp.where(back <= h0, below, above)
                here[...] = jnp.where(mine, self.held[self.z, sub], other)
                for side in (0, 1):
                    self.go(side, self.hops[side], sub, here, here)
            if k > h0:
                for side in (0, 1):
                    h = self.hops[side]
                    j = k - h0 - 1
                    if j >= h:
                        continue
                    p = self.came_piece(side, j)
                    block = self.full.at[p, sub]
                    self.came(side, h + j, sub, block)
                    if j + 1 < h:
                        self.go(side, h + j + 1, sub, block, block)
        if k == h0:
            self.landed(self.z)
        if k > h0:
            for side in (0, 1):
                j = k - h0 - 1
                if j < self.hops[side]:
                    self.landed(self.came_piece(side, j))

    def came_piece(self, side, j):
        return self.wrap(self.z - 1 - j if side == 0 else self.z + 1 + j)

    def steps(self):
        return 2 * self.hops[0] + 1

    def drain(self):
        for copy in self.flying.values():
            copy.wait_send()


def body(
    n_dp,
    owners,
    acts,
    grads,
    held_in_hbm,
    held_out_hbm,
    eig_hbm,
    out_hbm,
    all_acts,
    all_grads,
    all_rot,
    held_in,
    held_out,
    full_in,
    full_out,
    got_in,
    got_out,
    sum_in,
    sum_out,
    eig,
    out,
    send_sems,
    recv_sems,
    load_sems,
):
    z = lax.axis_index("dp")
    t = lax.axis_index("tensor")
    c = lax.rem(t, 2)
    x = lax.rem(lax.div(t, 2), NX)
    y = lax.div(t, 2 * NX)

    def chip(yy, xx, cc):
        return (z, (lax.rem(yy + NY, NY) * NX + lax.rem(xx + NX, NX)) * 2 + cc)

    to = {
        "+x": chip(y, x + 1, c),
        "-x": chip(y, x - 1, c),
        "+y": chip(y + 1, x, c),
        "-y": chip(y - 1, x, c),
        "core": chip(y, x, 1 - c),
    }
    up = (lax.rem(z + 1, n_dp), t)
    down = (lax.rem(z + n_dp - 1, n_dp), t)

    loads = [
        pltpu.make_async_copy(held_in_hbm, held_in, load_sems.at[0]),
        pltpu.make_async_copy(acts, all_acts.at[y, x, c], load_sems.at[1]),
        pltpu.make_async_copy(held_out_hbm, held_out, load_sems.at[2]),
        pltpu.make_async_copy(grads, all_grads.at[y, x, c], load_sems.at[3]),
        pltpu.make_async_copy(eig_hbm, eig, load_sems.at[4]),
    ]
    for load in loads:
        load.start()

    barrier = pltpu.get_barrier_semaphore()
    around = list(to.values()) + [up, down]
    for device in around:
        pl.semaphore_signal(barrier, inc=1, device_id=device, device_id_type=MESH)
    pl.semaphore_wait(barrier, len(around))

    send, recv = Slots(send_sems), Slots(recv_sems)
    acts_plane = Plane(all_acts, (y, x, c), to, send, recv)
    grads_plane = Plane(all_grads, (y, x, c), to, send, recv)
    rot_plane = Plane(all_rot, (y, x, c), to, send, recv)
    chunk = lambda ref, p, core: ref[lax.div(p, NX), lax.rem(p, NX), core].reshape(-1, ref.shape[-1])

    def add_to(total, ref, full):
        def landed(p):
            left = jnp.concatenate([chunk(ref, p, 0), chunk(ref, p, 1)], axis=1)
            right = full[p].reshape(-1, full.shape[-1])
            total[...] += jnp.dot(left, right, preferred_element_type=jnp.float32)

        return landed

    ring_in = Ring(
        n_dp, z, held_in, full_in, got_in, owners[0, t], up, down, send, recv, add_to(sum_in, all_acts, full_in)
    )
    ring_out = Ring(
        n_dp, z, held_out, full_out, got_out, owners[1, t], up, down, send, recv, add_to(sum_out, all_grads, full_out)
    )
    sum_in[...] = jnp.zeros_like(sum_in)
    sum_out[...] = jnp.zeros_like(sum_out)

    aw, gw, rw = acts_plane.waves(), grads_plane.waves(), rot_plane.waves()
    extra = {0: [1], 2: [2], 4: [3], 6: [4], 7: [5, 6]}
    extra_g = {3: [1], 6: [2], 9: [3], 12: [4], 14: [5, 6]}
    loads[0].wait()
    loads[1].wait()
    for k in range(ring_in.steps()):
        if k == 1:
            loads[2].wait()
        if k == 3:
            loads[3].wait()
        ring_in.step(k)
        if k % 2 == 1:
            ring_out.step(k // 2)
        for w in extra.get(k, ()):
            aw[w - 1]()
        for w in extra_g.get(k, ()):
            gw[w - 1]()

    rot = sum_in[...].astype(jnp.bfloat16)
    all_rot.at[y, x, c][...] = rot.reshape(all_rot.shape[3:])
    rw[0]()
    k = 8
    for w in (1, 2, 3, 4, 5):
        for _ in range(2):
            if k < ring_out.steps():
                ring_out.step(k)
                k += 1
        if w < 5:
            rw[w]()
    loads[4].wait()

    turned = jnp.transpose(sum_out[...]).astype(jnp.bfloat16)
    rw[5]()
    tokens = float(sum_in.shape[0])
    for p in range(NX * NY):
        right = jnp.concatenate([chunk(all_rot, p, 0), chunk(all_rot, p, 1)], axis=1)
        product = jnp.dot(turned, right, preferred_element_type=jnp.float32) / tokens
        cols = pl.ds(p * right.shape[1], right.shape[1])
        out[:, cols] = (product / (eig[:, cols].astype(jnp.float32) + damping)).astype(jnp.bfloat16)
    store = pltpu.make_async_copy(out, out_hbm, load_sems.at[5])
    store.start()
    for user in (acts_plane, grads_plane, rot_plane, ring_in, ring_out):
        user.drain()
    store.wait()


def shards(n_dp, acts, grads, basis_in_held, basis_out_held, owners, eig_lambda):
    tok, width = acts.shape[1:]
    depth = basis_in_held.shape[1]
    rows = depth // n_dp // SUBS
    slice_shape = (2, 2, tok // 4, width)
    held_shape = (n_dp, SUBS, rows, width)
    any_space = pl.BlockSpec(memory_space=pl.ANY)
    bf16, f32 = jnp.bfloat16, jnp.float32
    out = pl.pallas_call(
        functools.partial(body, n_dp),
        out_shape=jax.ShapeDtypeStruct(eig_lambda.shape, bf16),
        in_specs=[pl.BlockSpec(memory_space=pltpu.SMEM)] + [any_space] * 5,
        out_specs=any_space,
        scratch_shapes=[
            pltpu.VMEM((NY, NX, 2) + slice_shape, bf16),
            pltpu.VMEM((NY, NX, 2) + slice_shape, bf16),
            pltpu.VMEM((NY, NX, 2) + slice_shape, bf16),
            pltpu.VMEM(held_shape, bf16),
            pltpu.VMEM(held_shape, bf16),
            pltpu.VMEM(held_shape, bf16),
            pltpu.VMEM(held_shape, bf16),
            pltpu.VMEM((n_dp - 1,) + held_shape[1:], bf16),
            pltpu.VMEM((n_dp - 1,) + held_shape[1:], bf16),
            pltpu.VMEM((tok, width), f32),
            pltpu.VMEM((tok, width), f32),
            pltpu.VMEM(eig_lambda.shape, bf16),
            pltpu.VMEM(eig_lambda.shape, bf16),
            pltpu.SemaphoreType.DMA((152,)),
            pltpu.SemaphoreType.DMA((144 + 4 * (n_dp - 1) * SUBS,)),
            pltpu.SemaphoreType.DMA((6,)),
        ],
        compiler_params=pltpu.CompilerParams(
            collective_id=0, has_side_effects=True, vmem_limit_bytes=56 * 1024 * 1024
        ),
    )(
        owners,
        acts[0].reshape(slice_shape),
        grads[0].reshape(slice_shape),
        basis_in_held[0].reshape(held_shape),
        basis_out_held[0].reshape(held_shape),
        eig_lambda,
    )
    return out[None]


def solution(mesh):
    placed = (
        P("dp", None, "tensor"),
        P("dp", None, "tensor"),
        P("dp", None, "tensor"),
        P("dp", None, "tensor"),
        P(),
        P("tensor", None),
    )
    return jax.shard_map(
        functools.partial(shards, mesh.shape["dp"]),
        mesh=mesh,
        in_specs=placed,
        out_specs=P("dp", "tensor", None),
        check_vma=False,
    )
```

time: 240 us -> 100 us (0.42)
  waiting for transfers between devices: 209 us -> 0 us
  Pallas kernels: 0 us -> 97.7 us
  between operations: 16.3 us -> 0.01 us
  matrix products: 12.1 us -> 0 us
    psum x1 -> x0, waiting for transfers between devices: 141 us -> none  [from_root(): return lax.psum(block, axis)]
    pallas_call x0 -> x1, Pallas kernels: none -> 97.7 us  [shards(): pl.pallas_call(functools.partial(body, n_dp), out_shape=jax.ShapeDtypeStr...]
    all_gather x3 -> x0, waiting for transfers between devices: 66.9 us -> none  [the longest x1 66.8 us: shards(): lax.all_gather(rot_in, 'tensor', axis=1, tiled=True)]
    dot_general x2 -> x0, matrix products: 12.1 us -> none  [the longest x1 7.36 us: shards(): lax.dot_general(rot_out, lax.all_gather(rot_in, 'tensor', axis=1, tiled=T...]
  transfers between devices with their start and end apart: 4 -> 0, of which waited for: 2 -> 0; matrix products, arithmetic and copies ran while one was open for 2% -> 0% of each run, Pallas kernels for 0% -> 0%
where the time goes in v1:
time: 100 us
  Pallas kernels  97.7 us (98%)
  local copies, waits for them, and re-layouts  2.29 us (2%)
    pallas_call x1, Pallas kernels, shards(): pl.pallas_call(functools.partial(body, n_dp), out_shape=jax.ShapeDtypeStr...  97.7 us
    unnamed x1, local copies, waits for them, and re-layouts  2.29 us

profile of v1, /device:TPU:1, one launch (start us, length us, event | category | flops | bytes accessed | tf_op | source)
XLA Modules:
  0.0 100.0 jit_solution(11745581144214687724)
XLA Ops:
  0.0 97.7 %shard_map.64 = bf16[128,4096]{1,0:T(8,128)(2,1)} custom-call(s32[2,32]{1,0:T(2,128)} %owners.1, bf16[2,2,128,128]{3,2,1,0:T(8,128)(2,1)} %bitcast.8, bf16[2,2,128,128]{3,2,1,0:T(8,128)(2,1)} %bitcast.9, bf16[16,2,128,128]{3,2,1,0:T(8,128)(2,1)} %bitcast.6, bf16[16,2,128,128]{3,2,1,0:T(8,128)(2,1)} %bitcast.7, bf16[128,4096]{1,0:T(8,128)(2,1)} %eig_hbm.1), custom_call_target="tpu_custom_call" | custom-call | tf_op jit(solution)/shard_map/pallas_call | solution.py:395
  97.7 2.3 %copy.8 = bf16[1,128,4096]{2,1,0:T(8,128)(2,1)} copy(bf16[1,128,4096]{2,1,0:T(8,128)(2,1)} %bitcast.5) | data formatting | bytes 2097152

commit v2 on v0

v2 whole, which is shorter than its diff:
```python
import functools

import jax
import jax.numpy as jnp
from jax import lax
from jax.experimental import pallas as pl
from jax.experimental.pallas import tpu as pltpu
from jax.sharding import PartitionSpec as P

damping = 0.01
MESH = pl.DeviceIdType.MESH
NX = 4
NY = 4
SUBS = 2
ORDER = (
    "i0 o0 a1 e0", "i1 o1 i2 o2", "a2 i3 o3 i4", "o4 a3 i5 o5", "a4 i6 o6 a5", "a6 g1 i7 o7",
    "i8 o8 g2 i9", "o9 i10 o10 g3", "i11 o11 g4 i12", "o12 r1 g5 g6", "o13 r2 o14 r3", "o15 r4 o16 t0",
    "r5",
)


class Slots:
    def __init__(self, sems):
        self.sems = sems
        self.used = 0

    def take(self):
        self.used += 1
        return self.sems.at[self.used - 1]


class Plane:
    WAYS = {"x2": (2, 0), "+x": (1, 0), "-x": (-1, 0), "y2": (0, 2), "+y": (0, 1), "-y": (0, -1)}
    NEAR = ((-1, 0), (1, 0), (0, -1), (0, 1))
    AXES = ((2, 0), (0, 2))
    CORNERS = ((-1, -1), (1, -1), (-1, 1), (1, 1), (-1, 2), (1, 2), (2, -1), (2, 1), (2, 2))

    def __init__(self, buf, where, to, send, recv):
        self.buf, self.to, self.send, self.recv = buf, to, send, recv
        self.y, self.x, self.c = where
        self.landing = {}
        self.partner = {}
        self.sent = []

    def chip(self, dx, dy):
        return lax.rem(self.y + (dy % NY), NY), lax.rem(self.x + (dx % NX), NX)

    def move(self, way, region, lands):
        recv = self.recv.take()
        copy = pltpu.make_async_remote_copy(
            region, region, self.send.take(), recv, device_id=self.to[way], device_id_type=MESH
        )
        copy.start()
        self.sent.append(copy)
        return pltpu.make_async_remote_copy(
            lands, lands, self.send.sems.at[0], recv, device_id=self.to[way], device_id_type=MESH
        )

    def push(self, way, dx, dy, part):
        wx, wy = self.WAYS[way]
        there = ((dx - wx) % NX, (dy - wy) % NY)
        region = self.buf.at[self.chip(dx, dy) + (self.c,) + part]
        lands = self.buf.at[self.chip(*there) + (self.c,) + part]
        self.landing[(there, part)] = self.move(way, region, lands)

    def arrive(self, dx, dy, part):
        self.landing.pop(((dx % NX, dy % NY), part)).wait_recv()

    def share(self, dx, dy):
        region = self.buf.at[self.chip(dx, dy) + (self.c,)]
        lands = self.buf.at[self.chip(dx, dy) + (1 - self.c,)]
        self.partner[(dx % NX, dy % NY)] = self.move("core", region, lands)

    def whole(self, dx, dy):
        self.partner.pop((dx % NX, dy % NY)).wait_recv()

    def start(self):
        for first, second in ((0, 1), (1, 0)):
            for way in ("x2", "+x", "-x"):
                self.push(way, 0, 0, (first,))
            for way in ("y2", "+y", "-y"):
                self.push(way, 0, 0, (second,))
        self.share(0, 0)

    def onward(self, places):
        for dx, dy in places:
            part = (0,) if dx else (1,)
            self.arrive(dx, dy, part)
            for side in ("y2", "+y", "-y") if dx else ("x2", "+x", "-x"):
                self.push(side, dx, dy, part)

    def fill(self, places):
        for dx, dy in places:
            self.arrive(dx, dy, (1,) if dx else (0,))
            self.share(dx, dy)

    def corners(self, places):
        for dx, dy in places:
            self.arrive(dx, dy, (0,))
            self.arrive(dx, dy, (1,))
            self.share(dx, dy)

    def wave(self, number):
        if number == 1:
            self.start()
        elif number == 2:
            self.onward(self.NEAR)
        elif number == 3:
            self.onward(self.AXES)
            self.fill(self.NEAR + self.AXES)
        elif number == 4:
            self.corners(self.CORNERS[:4])
        elif number == 5:
            self.corners(self.CORNERS[4:])
        else:
            for dx, dy in list(self.partner):
                self.whole(dx, dy)

    def drain(self):
        for copy in self.sent:
            copy.wait_send()


class Ring:
    def __init__(self, n, z, t, held, full, got, owner, flows, send, recv, landed):
        self.n, self.z, self.t, self.held, self.full, self.got = n, z, t, held, full, got
        self.owner, self.flows, self.landed = owner, flows, landed
        self.most = max(hops for _, _, hops in flows)
        self.base = [sum(h for _, _, h in flows[:i]) for i in range(len(flows))]
        self.recv = [[[recv.take() for _ in range(SUBS)] for _ in range(2 * h)] for _, _, h in flows]
        self.send = [[[send.take() for _ in range(SUBS)] for _ in range(2 * h)] for _, _, h in flows]
        self.sent = []
        self.ready = []

    def wrap(self, p):
        return lax.rem(p + 4 * self.n, self.n)

    def copy(self, f, step, sub, src, dst):
        sign, base, hops = self.flows[f]
        away = base + 1 if step in (hops - 1, hops) else 1
        return pltpu.make_async_remote_copy(
            src,
            dst,
            self.send[f][step][sub],
            self.recv[f][step][sub],
            device_id=(self.wrap(self.z + sign * away), self.t),
            device_id_type=MESH,
        )

    def go(self, f, step, sub, src, dst):
        copy = self.copy(f, step, sub, src, dst)
        copy.start()
        self.sent.append(copy)

    def came(self, f, step, sub, where):
        self.copy(f, step, sub, where, where).wait_recv()

    def slot(self, f, step, sub):
        return self.got.at[self.base[f] + step, sub]

    def spread(self, f, j):
        sign, base, _ = self.flows[f]
        return self.wrap(self.z - sign * (base + 1 + j))

    def combine(self, sub):
        back = self.z - self.owner
        back = jnp.where(back < 0, back + self.n, back)
        best = self.held[self.z, sub]
        for f, (sign, base, hops) in enumerate(self.flows):
            slot = self.slot(f, hops - 1, sub)
            self.came(f, hops - 1, sub, slot)
            far = back if sign > 0 else self.n - back
            best = jnp.where(jnp.logical_and(far > base, far <= base + hops), slot[...], best)
        here = self.full.at[self.z, sub]
        here[...] = best
        for f, (_, _, hops) in enumerate(self.flows):
            self.go(f, hops, sub, here, here)

    def step(self, k):
        mine = self.owner == self.z
        flows = sorted(range(len(self.flows)), key=lambda f: -self.flows[f][1])
        for sub in range(SUBS):
            if k == self.most:
                self.combine(sub)
            for f in flows:
                sign, base, hops = self.flows[f]
                if k < hops:
                    src = self.held.at[self.wrap(self.z + sign * (base + hops - k)), sub]
                    if k > 0:
                        slot = self.slot(f, k - 1, sub)
                        self.came(f, k - 1, sub, slot)
                        slot[...] = jnp.where(mine, src[...], slot[...])
                        src = slot
                    self.go(f, k, sub, src, self.slot(f, k, sub))
                j = k - self.most - 1
                if 0 <= j < hops:
                    block = self.full.at[self.spread(f, j), sub]
                    self.came(f, hops + j, sub, block)
                    if j + 1 < hops:
                        self.go(f, hops + j + 1, sub, block, block)
        if k == self.most:
            self.ready.append(self.z)
        for f, (_, _, hops) in enumerate(self.flows):
            if 0 <= k - self.most - 1 < hops:
                self.ready.append(self.spread(f, k - self.most - 1))

    def flush(self):
        for p in self.ready:
            self.landed(p)
        self.ready = []

    def drain(self):
        for copy in self.sent:
            copy.wait_send()


def body(
    n_dp,
    owners,
    acts,
    grads,
    held_in_hbm,
    held_out_hbm,
    eig_hbm,
    out_hbm,
    all_acts,
    all_grads,
    all_rot,
    held_in,
    held_out,
    full_in,
    full_out,
    got_in,
    got_out,
    sum_in,
    sum_out,
    eig,
    scale,
    out,
    send_sems,
    recv_sems,
    load_sems,
):
    z = lax.axis_index("dp")
    t = lax.axis_index("tensor")
    c = lax.rem(t, 2)
    x = lax.rem(lax.div(t, 2), NX)
    y = lax.div(t, 2 * NX)

    def chip(yy, xx, cc):
        return (z, (lax.rem(yy + NY, NY) * NX + lax.rem(xx + NX, NX)) * 2 + cc)

    to = {
        "+x": chip(y, x + 1, c),
        "-x": chip(y, x - 1, c),
        "+y": chip(y + 1, x, c),
        "-y": chip(y - 1, x, c),
        "x2": chip(y, x + 2, c),
        "y2": chip(y + 2, x, c),
        "core": chip(y, x, 1 - c),
    }
    in_flows = ((1, 0, 2), (1, 2, 6), (-1, 0, 2), (-1, 2, 5))
    out_flows = ((1, 0, 8), (-1, 0, 7))
    reach = sorted({sign * (base + 1) for sign, base, _ in in_flows + out_flows})

    loads = [
        pltpu.make_async_copy(held_in_hbm, held_in, load_sems.at[0]),
        pltpu.make_async_copy(acts, all_acts.at[y, x, c], load_sems.at[1]),
        pltpu.make_async_copy(held_out_hbm, held_out, load_sems.at[2]),
        pltpu.make_async_copy(grads, all_grads.at[y, x, c], load_sems.at[3]),
        pltpu.make_async_copy(eig_hbm, eig, load_sems.at[4]),
    ]
    for load in loads:
        load.start()

    barrier = pltpu.get_barrier_semaphore()
    around = list(to.values()) + [(lax.rem(z + n_dp + far, n_dp), t) for far in sorted(reach + [-far for far in reach if -far not in reach])]
    for device in around:
        pl.semaphore_signal(barrier, inc=1, device_id=device, device_id_type=MESH)
    pl.semaphore_wait(barrier, len(around))

    send, recv = Slots(send_sems), Slots(recv_sems)
    acts_plane = Plane(all_acts, (y, x, c), to, send, recv)
    grads_plane = Plane(all_grads, (y, x, c), to, send, recv)
    rot_plane = Plane(all_rot, (y, x, c), to, send, recv)
    chunk = lambda ref, p, core: ref[lax.div(p, NX), lax.rem(p, NX), core].reshape(-1, ref.shape[-1])

    def add_to(total, ref, full):
        def landed(p):
            left = jnp.concatenate([chunk(ref, p, 0), chunk(ref, p, 1)], axis=1)
            right = full[p].reshape(-1, full.shape[-1])
            total[...] += jnp.dot(left, right, preferred_element_type=jnp.float32)

        return landed

    ring_in = Ring(
        n_dp, z, t, held_in, full_in, got_in, owners[0, t], in_flows, send, recv, add_to(sum_in, all_acts, full_in)
    )
    ring_out = Ring(
        n_dp, z, t, held_out, full_out, got_out, owners[1, t], out_flows, send, recv, add_to(sum_out, all_grads, full_out)
    )
    for load in loads:
        load.wait()
    done = set()
    for word in " ".join(ORDER).split():
        kind, number = word[0], int(word[1:])
        if kind == "i":
            ring_in.step(number)
        elif kind == "o":
            ring_out.step(number)
        elif kind == "a":
            acts_plane.wave(number)
        elif kind == "g":
            grads_plane.wave(number)
        elif kind == "r":
            if number == 1:
                rot = sum_in[...].astype(jnp.bfloat16)
                all_rot.at[y, x, c][...] = rot.reshape(all_rot.shape[3:])
            rot_plane.wave(number)
        elif kind == "e":
            scale[...] = 1.0 / (eig[...].astype(jnp.float32) + damping)
            sum_in[...] = jnp.zeros_like(sum_in)
            sum_out[...] = jnp.zeros_like(sum_out)
        else:
            turned = jnp.transpose(sum_out[...]).astype(jnp.bfloat16)
        done.add(word)
        if "a6" in done:
            ring_in.flush()
        if "g6" in done:
            ring_out.flush()

    tokens = sum_in.shape[0]
    stores = []
    for i, (dx, dy) in enumerate(((0, 0),) + Plane.NEAR + Plane.AXES + Plane.CORNERS):
        rot_plane.whole(dx, dy)
        p = lax.rem(y + (dy % NY), NY) * NX + lax.rem(x + (dx % NX), NX)
        right = jnp.concatenate([chunk(all_rot, p, 0), chunk(all_rot, p, 1)], axis=1)
        cols = pl.ds(pl.multiple_of(p * right.shape[1], right.shape[1]), right.shape[1])
        product = jnp.dot(turned, right, preferred_element_type=jnp.float32) * (1.0 / tokens)
        out[:, cols] = (product * scale[:, cols]).astype(jnp.bfloat16)
        stores.append(pltpu.make_async_copy(out.at[:, cols], out_hbm.at[:, cols], load_sems.at[5 + i]))
        stores[-1].start()
    for user in (acts_plane, grads_plane, rot_plane, ring_in, ring_out):
        user.drain()
    for store in stores:
        store.wait()


def shards(n_dp, acts, grads, basis_in_held, basis_out_held, owners, eig_lambda):
    tok, width = acts.shape[1:]
    depth = basis_in_held.shape[1]
    rows = depth // n_dp // SUBS
    slice_shape = (2, tok // 2, width)
    held_shape = (n_dp, SUBS, rows, width)
    any_space = pl.BlockSpec(memory_space=pl.ANY)
    bf16, f32 = jnp.bfloat16, jnp.float32
    out = pl.pallas_call(
        functools.partial(body, n_dp),
        out_shape=jax.ShapeDtypeStruct(eig_lambda.shape, bf16),
        in_specs=[pl.BlockSpec(memory_space=pltpu.SMEM)] + [any_space] * 5,
        out_specs=any_space,
        scratch_shapes=[
            pltpu.VMEM((NY, NX, 2) + slice_shape, bf16),
            pltpu.VMEM((NY, NX, 2) + slice_shape, bf16),
            pltpu.VMEM((NY, NX, 2) + slice_shape, bf16),
            pltpu.VMEM(held_shape, bf16),
            pltpu.VMEM(held_shape, bf16),
            pltpu.VMEM(held_shape, bf16),
            pltpu.VMEM(held_shape, bf16),
            pltpu.VMEM((n_dp - 1,) + held_shape[1:], bf16),
            pltpu.VMEM((n_dp - 1,) + held_shape[1:], bf16),
            pltpu.VMEM((tok, width), f32),
            pltpu.VMEM((tok, width), f32),
            pltpu.VMEM(eig_lambda.shape, bf16),
            pltpu.VMEM(eig_lambda.shape, f32),
            pltpu.VMEM(eig_lambda.shape, bf16),
            pltpu.SemaphoreType.DMA((138 + 4 * (n_dp - 1) * SUBS,)),
            pltpu.SemaphoreType.DMA((138 + 4 * (n_dp - 1) * SUBS,)),
            pltpu.SemaphoreType.DMA((5 + NX * NY,)),
        ],
        compiler_params=pltpu.CompilerParams(
            collective_id=0, has_side_effects=True, vmem_limit_bytes=56 * 1024 * 1024
        ),
    )(
        owners,
        acts[0].reshape(slice_shape),
        grads[0].reshape(slice_shape),
        basis_in_held[0].reshape(held_shape),
        basis_out_held[0].reshape(held_shape),
        eig_lambda,
    )
    return out[None]


def solution(mesh):
    placed = (
        P("dp", None, "tensor"),
        P("dp", None, "tensor"),
        P("dp", None, "tensor"),
        P("dp", None, "tensor"),
        P(),
        P("tensor", None),
    )
    return jax.shard_map(
        functools.partial(shards, mesh.shape["dp"]),
        mesh=mesh,
        in_specs=placed,
        out_specs=P("dp", "tensor", None),
        check_vma=False,
    )
```

time: 240 us -> 91.3 us (0.38)
  waiting for transfers between devices: 209 us -> 0 us
  Pallas kernels: 0 us -> 88.8 us
  between operations: 16.3 us -> 0.01 us
  matrix products: 12.1 us -> 0 us
    psum x1 -> x0, waiting for transfers between devices: 141 us -> none  [from_root(): return lax.psum(block, axis)]
    pallas_call x0 -> x1, Pallas kernels: none -> 88.8 us  [shards(): pl.pallas_call(functools.partial(body, n_dp), out_shape=jax.ShapeDtypeStr...]
    all_gather x3 -> x0, waiting for transfers between devices: 66.9 us -> none  [the longest x1 66.8 us: shards(): lax.all_gather(rot_in, 'tensor', axis=1, tiled=True)]
    dot_general x2 -> x0, matrix products: 12.1 us -> none  [the longest x1 7.36 us: shards(): lax.dot_general(rot_out, lax.all_gather(rot_in, 'tensor', axis=1, tiled=T...]
  transfers between devices with their start and end apart: 4 -> 0, of which waited for: 2 -> 0; matrix products, arithmetic and copies ran while one was open for 2% -> 0% of each run, Pallas kernels for 0% -> 0%
where the time goes in v2:
time: 91.3 us; the launch traced here: 91.1 us
  Pallas kernels  88.8 us (97%)
  local copies, waits for them, and re-layouts  2.29 us (3%)
    pallas_call x1, Pallas kernels, shards(): pl.pallas_call(functools.partial(body, n_dp), out_shape=jax.ShapeDtypeStr...  88.8 us
    unnamed x1, local copies, waits for them, and re-layouts  2.29 us

profile of v2, /device:TPU:1, one launch (start us, length us, event | category | flops | bytes accessed | tf_op | source)
XLA Modules:
  0.0 91.1 jit_solution(14091133328376857452)
XLA Ops:
  0.0 88.8 %shard_map.64 = bf16[128,4096]{1,0:T(8,128)(2,1)} custom-call(s32[2,32]{1,0:T(2,128)} %owners.1, bf16[2,256,128]{2,1,0:T(8,128)(2,1)} %bitcast.8, bf16[2,256,128]{2,1,0:T(8,128)(2,1)} %bitcast.9, bf16[16,2,128,128]{3,2,1,0:T(8,128)(2,1)} %bitcast.6, bf16[16,2,128,128]{3,2,1,0:T(8,128)(2,1)} %bitcast.7, bf16[128,4096]{1,0:T(8,128)(2,1)} %eig_hbm.1), custom_call_target="tpu_custom_call" | custom-call | tf_op jit(solution)/shard_map/pallas_call | solution.py:357
  88.8 2.3 %copy.8 = bf16[1,128,4096]{2,1,0:T(8,128)(2,1)} copy(bf16[1,128,4096]{2,1,0:T(8,128)(2,1)} %bitcast.5) | data formatting | bytes 2097152

commit v3 on v2

--- a/solution.py
+++ b/solution.py
@@ -323,6 +323,8 @@
             sum_out[...] = jnp.zeros_like(sum_out)
         else:
             turned = jnp.transpose(sum_out[...]).astype(jnp.bfloat16)
+            for user in (acts_plane, grads_plane, ring_in, ring_out):
+                user.drain()
         done.add(word)
         if "a6" in done:
             ring_in.flush()
@@ -340,8 +342,7 @@
         out[:, cols] = (product * scale[:, cols]).astype(jnp.bfloat16)
         stores.append(pltpu.make_async_copy(out.at[:, cols], out_hbm.at[:, cols], load_sems.at[5 + i]))
         stores[-1].start()
-    for user in (acts_plane, grads_plane, rot_plane, ring_in, ring_out):
-        user.drain()
+    rot_plane.drain()
     for store in stores:
         store.wait()
 

time: 91.3 us -> 91.3 us (level)
  no operation moved by 1% of the time
where the time goes in v3:
time: 91.3 us; the launch traced here: 91.1 us
  Pallas kernels  88.8 us (97%)
  local copies, waits for them, and re-layouts  2.29 us (3%)
    pallas_call x1, Pallas kernels, shards(): pl.pallas_call(functools.partial(body, n_dp), out_shape=jax.ShapeDtypeStr...  88.8 us
    unnamed x1, local copies, waits for them, and re-layouts  2.29 us

profile of v3, /device:TPU:1, one launch (start us, length us, event | category | flops | bytes accessed | tf_op | source)
XLA Modules:
  0.0 91.1 jit_solution(9626091822228648140)
XLA Ops:
  0.0 88.8 %shard_map.64 = bf16[128,4096]{1,0:T(8,128)(2,1)} custom-call(s32[2,32]{1,0:T(2,128)} %owners.1, bf16[2,256,128]{2,1,0:T(8,128)(2,1)} %bitcast.8, bf16[2,256,128]{2,1,0:T(8,128)(2,1)} %bitcast.9, bf16[16,2,128,128]{3,2,1,0:T(8,128)(2,1)} %bitcast.6, bf16[16,2,128,128]{3,2,1,0:T(8,128)(2,1)} %bitcast.7, bf16[128,4096]{1,0:T(8,128)(2,1)} %eig_hbm.1), custom_call_target="tpu_custom_call" | custom-call | tf_op jit(solution)/shard_map/pallas_call | solution.py:358
  88.8 2.3 %copy.8 = bf16[1,128,4096]{2,1,0:T(8,128)(2,1)} copy(bf16[1,128,4096]{2,1,0:T(8,128)(2,1)} %bitcast.5) | data formatting | bytes 2097152
